TPU v7x, 512 devices: a whole 4x4x16 slice. The times are simulated.
512 devices in a mesh: tile: 128 (over z, y, core), fac: 4 (over x).
Axes of the slice: x: 4, y: 4, z: 16, core: 2. Of those that a mesh axis runs over, the one named last changes fastest.
Arguments:
- panel: float32 [64, 1024, 2048], P('fac', 'tile'), may hold values from -7000 to 7000
- materials: int32 [1024, 2048], P('tile'), may hold values from 0 to 7
- table: float32 [4, 8], replicated, may hold values from 0.2 to 5
- shifts: float32 [8], replicated, may hold values from 0.05 to 0.5
- shift_pick: int32 [1], replicated, may hold values from 0 to 7
Outputs:
- basis: float32 [64, 1024, 2048], P('fac', 'tile')
All inputs are finite; a program needn't handle non-finite values.
Results may differ from a plain program's by a relative error of at most 0.0003.
Values sent between devices are 32-bit elements; how exact they have to be, the bound alone decides.
A program may use at most 64 MiB of HBM per device.

v0:
```python
import jax
import jax.numpy as jnp
from jax import lax
from jax.sharding import PartitionSpec as P

NZ = 64
SWEEPS = 4
OMEGA = 0.8


def padded(value, sides, width):
    for axis, dim in sides:
        count, length = (lax.axis_size(axis), value.shape[dim])
        up = [(i, (i + 1) % count) for i in range(count - 1)]
        down = [(j, i) for i, j in up]
        last = lax.slice_in_dim(value, length - width, length, axis=dim)
        initial = lax.slice_in_dim(value, 0, width, axis=dim)
        before = lax.ppermute(last, axis, up)
        after = lax.ppermute(initial, axis, down)
        value = jnp.concatenate([before, value, after], axis=dim)
    return value


def swapped(value, axis, apart):
    return lax.ppermute(value, axis, [(i, i ^ 1 << apart) for i in range(lax.axis_size(axis))])


def harmonic(first, second):
    total = first + second
    safe = jnp.where(total > 0, total, 1.0)
    return 2.0 * first * second / safe


def material_fields(materials, table):
    fields = jnp.zeros((4,) + materials.shape, jnp.float32)
    for index in range(table.shape[1]):
        fields = fields + jnp.where(materials[None] == index, table[:, index][:, None, None], 0.0)
    return fields


def coefficients(fields, shift_value):
    cond_x = fields[0]
    faces_x = harmonic(cond_x[:-1], cond_x[1:])
    prev_x = faces_x[:-1]
    next_x = faces_x[1:]
    inner = fields[:, 1:-1]
    cond_y = inner[1]
    cond_z = inner[2]
    capacity = inner[3]
    count = cond_y.shape[0]
    width = cond_y.shape[1]
    zeros_y = jnp.zeros((count, NZ), jnp.float32)
    zeros_z = jnp.zeros((count, 1), jnp.float32)
    upper_y = jnp.concatenate([cond_y[:, NZ:], zeros_y], 1)
    next_y = harmonic(cond_y, upper_y)
    prev_y = jnp.concatenate([zeros_y, next_y[:, :-NZ]], 1)
    layer = jnp.arange(width) % NZ
    upper_z = jnp.concatenate([cond_z[:, 1:], zeros_z], 1)
    upper_z = jnp.where(layer[None] < NZ - 1, upper_z, 0.0)
    next_z = harmonic(cond_z, upper_z)
    prev_z = jnp.concatenate([zeros_z, next_z[:, :-1]], 1)
    diagonal = shift_value * capacity + prev_x + next_x + prev_y + next_y + prev_z + next_z
    inverse = jnp.where(capacity > 0, 1.0 / jnp.where(capacity > 0, diagonal, 1.0), 0.0)
    return (prev_x, next_x, prev_y, next_y, prev_z, next_z, inverse)


def relax(extended, source, coeffs):
    prev_x, next_x, prev_y, next_y, prev_z, next_z, inverse = coeffs
    center = extended[:, 1:-1]
    shape_y = center.shape[:-1] + (NZ,)
    shape_z = center.shape[:-1] + (1,)
    up_y = jnp.concatenate([center[..., NZ:], jnp.zeros(shape_y, center.dtype)], -1)
    down_y = jnp.concatenate([jnp.zeros(shape_y, center.dtype), center[..., :-NZ]], -1)
    up_z = jnp.concatenate([center[..., 1:], jnp.zeros(shape_z, center.dtype)], -1)
    down_z = jnp.concatenate([jnp.zeros(shape_z, center.dtype), center[..., :-1]], -1)
    beside = prev_x * extended[:, :-2] + next_x * extended[:, 2:]
    beside = beside + next_y * up_y + prev_y * down_y + next_z * up_z + prev_z * down_z
    return (1.0 - OMEGA) * center + OMEGA * (source + beside) * inverse


def gram_of(matrix):
    return jnp.dot(
        matrix, matrix.T, precision=lax.Precision.HIGHEST, preferred_element_type=jnp.float32
    )


def per_device(panel, materials, table, shifts, shift_pick):
    picker = jnp.arange(shifts.shape[0]) == shift_pick[0]
    shift_value = jnp.sum(jnp.where(picker, shifts, 0.0))
    fields = material_fields(materials, table)
    fields_ext = padded(fields, (("tile", 1),), 1)
    coeffs = coefficients(fields_ext, shift_value)
    solution = panel * coeffs[6][None]
    for sweep_index in range(SWEEPS):
        extended = padded(solution, (("tile", 1),), 1)
        solution = relax(extended, panel, coeffs)
    own_cols = solution.shape[0]
    column_count = 2 * own_cols
    ncells = solution.shape[1] * lax.axis_size("tile") * solution.shape[2]
    position = lax.axis_index("fac")
    half_id = position % 2
    half_rows = solution.shape[1] // 2
    keeping = lax.dynamic_slice_in_dim(solution, half_id * half_rows, half_rows, 1)
    giving = lax.dynamic_slice_in_dim(solution, (1 - half_id) * half_rows, half_rows, 1)
    received = swapped(giving, "fac", 0)
    merged = jnp.where(
        half_id == 0,
        jnp.concatenate([keeping, received], 0),
        jnp.concatenate([received, keeping], 0),
    )
    matrix = merged.reshape(column_count, -1)
    partial_value = gram_of(matrix)
    tile_sum = lax.psum(partial_value, "tile")
    total = tile_sum + swapped(tile_sum, "fac", 0)
    lower_factor = jnp.linalg.cholesky(total / ncells)
    ortho = lax.linalg.triangular_solve(lower_factor, matrix, left_side=True, lower=True).reshape(
        merged.shape
    )
    mine = lax.dynamic_slice_in_dim(ortho, half_id * own_cols, own_cols, 0)
    theirs = lax.dynamic_slice_in_dim(ortho, (1 - half_id) * own_cols, own_cols, 0)
    returned = swapped(theirs, "fac", 0)
    result = jnp.where(
        half_id == 0, jnp.concatenate([mine, returned], 1), jnp.concatenate([returned, mine], 1)
    )
    return result


def solution(mesh):
    placed = (P("fac", "tile", None), P("tile", None), P(), P(), P())
    return jax.shard_map(
        per_device, mesh=mesh, in_specs=placed, out_specs=P("fac", "tile", None), check_vma=False
    )
```

profile of v0, /device:TPU:262, one launch (start us, length us, event | category | flops | bytes accessed | tf_op | source)
XLA Modules:
  0.0 602.3 jit_solution(5284592554948806002)
XLA Ops:
  1.6 1.9 collective-permute-start
  3.5 7.0 %collective-permute-start.1 = (f32[4,1,2048]{2,1,0:T(1,128)S(1)}, f32[4,1,2048]{2,1,0:T(1,128)S(1)}, u32[]{:S(2)}, u32[]{:S(2)}) collective-permute-start(f32[4,1,2048]{2,1,0:T(1,128)S(1)} %get-tuple-element.44), channel_id=1, source_target_pairs={{4,0},{8,4},{12,8},{16,12},{20,16},{24,20},{28,24},{32,28},{36,32}... | collective-permute-start | bytes 98312 | tf_op jit(solution)/shard_map/ppermute | solution.py:19
  13.9 1.9 collective-permute-start.2
  15.8 7.0 %collective-permute-start.3 = (f32[16,1,2048]{2,0,1:T(8,128)S(1)}, f32[16,1,2048]{2,0,1:T(8,128)S(1)}, u32[]{:S(2)}, u32[]{:S(2)}) collective-permute-start(f32[16,1,2048]{2,0,1:T(8,128)S(1)} %get-tuple-element.42), channel_id=1, source_target_pairs={{4,0},{8,4},{12,8},{16,12},{20,16},{24,20},{28,24},{32,28},{36,32}... | collective-permute-start | bytes 393224 | tf_op jit(solution)/shard_map/ppermute | solution.py:19
  23.5 1.8 collective-permute-done.3
  27.3 1.9 collective-permute-start.4
  29.2 7.1 %collective-permute-start.5 = (f32[16,1,2048]{2,0,1:T(8,128)S(1)}, f32[16,1,2048]{2,0,1:T(8,128)S(1)}, u32[]{:S(2)}, u32[]{:S(2)}) collective-permute-start(f32[16,1,2048]{2,0,1:T(8,128)S(1)} %get-tuple-element.36), channel_id=1, source_target_pairs={{4,0},{8,4},{12,8},{16,12},{20,16},{24,20},{28,24},{32,28},{36,32}... | collective-permute-start | bytes 393224 | tf_op jit(solution)/shard_map/ppermute | solution.py:19
  37.0 1.8 collective-permute-done.5
  40.8 1.9 collective-permute-start.6
  42.8 7.1 %collective-permute-start.7 = (f32[16,1,2048]{2,0,1:T(8,128)S(1)}, f32[16,1,2048]{2,0,1:T(8,128)S(1)}, u32[]{:S(2)}, u32[]{:S(2)}) collective-permute-start(f32[16,1,2048]{2,0,1:T(8,128)S(1)} %get-tuple-element.30), channel_id=1, source_target_pairs={{4,0},{8,4},{12,8},{16,12},{20,16},{24,20},{28,24},{32,28},{36,32}... | collective-permute-start | bytes 393224 | tf_op jit(solution)/shard_map/ppermute | solution.py:19
  50.6 1.8 collective-permute-done.7
  52.4 1.6 fusion.21
  54.4 1.9 collective-permute-start.8
  56.3 7.1 %collective-permute-start.9 = (f32[16,1,2048]{2,0,1:T(8,128)S(1)}, f32[16,1,2048]{2,0,1:T(8,128)S(1)}, u32[]{:S(2)}, u32[]{:S(2)}) collective-permute-start(f32[16,1,2048]{2,0,1:T(8,128)S(1)} %get-tuple-element.24), channel_id=1, source_target_pairs={{4,0},{8,4},{12,8},{16,12},{20,16},{24,20},{28,24},{32,28},{36,32}... | collective-permute-start | bytes 393224 | tf_op jit(solution)/shard_map/ppermute | solution.py:19
  64.1 1.8 collective-permute-done.9
  67.6 2.9 collective-permute-start.10
  70.6 8.1 %collective-permute-done.10 = f32[16,4,2048]{2,0,1:T(8,128)S(1)} collective-permute-done((f32[16,4,2048]{2,0,1:T(8,128)S(1)}, f32[16,4,2048]{2,0,1:T(8,128)S(1)}, u32[]{:S(2)}, u32[]{:S(2)}) %collective-permute-start.10) | collective-permute-done | bytes 524320 | tf_op jit(solution)/shard_map/ppermute | solution.py:25
  79.7 496.3 %psum.7 = f32[32,32]{0,1:T(8,128)S(1)} all-reduce(f32[32,32]{0,1:T(8,128)S(1)} %convolution_bitcast_fusion), channel_id=1, replica_groups=mesh['tile'=128,'fac'=4] {'tile'}, use_global_device_ids=true, to_apply=%region_1.2 | all-reduce | flops 1024 | bytes 8192 | tf_op jit(solution)/shard_map/psum | solution.py:113
  576.0 2.7 collective-permute-start.11
  578.9 2.8 collective-permute-done.11
  581.7 2.9 cholesky.16
  586.0 2.4 custom-call.6
  589.6 2.7 collective-permute-start.12
  592.3 8.3 %collective-permute-done.12 = f32[16,4,2048]{2,0,1:T(8,128)S(1)} collective-permute-done((f32[16,4,2048]{2,0,1:T(8,128)S(1)}, f32[16,4,2048]{2,0,1:T(8,128)S(1)}, u32[]{:S(2)}, u32[]{:S(2)}) %collective-permute-start.12) | collective-permute-done | bytes 524320 | tf_op jit(solution)/shard_map/ppermute | solution.py:25
  (55 shorter events, 18.3 us)
Async XLA Ops:
  0.0 0.9 copy-start.1
  1.6 10.5 %collective-permute-start = (f32[4,1,2048]{2,1,0:T(1,128)S(1)}, f32[4,1,2048]{2,1,0:T(1,128)S(1)}, u32[]{:S(2)}, u32[]{:S(2)}) collective-permute-start(f32[4,1,2048]{2,1,0:T(1,128)S(1)} %get-tuple-element.43), channel_id=1, source_target_pairs={{0,4},{4,8},{8,12},{12,16},{16,20},{20,24},{24,28},{28,32},{32,36}... | collective-permute-start | bytes 98312 | tf_op jit(solution)/shard_map/ppermute | solution.py:18
  3.5 8.6 %collective-permute-start.1 = (f32[4,1,2048]{2,1,0:T(1,128)S(1)}, f32[4,1,2048]{2,1,0:T(1,128)S(1)}, u32[]{:S(2)}, u32[]{:S(2)}) collective-permute-start(f32[4,1,2048]{2,1,0:T(1,128)S(1)} %get-tuple-element.44), channel_id=1, source_target_pairs={{4,0},{8,4},{12,8},{16,12},{20,16},{24,20},{28,24},{32,28},{36,32}... | collective-permute-start | bytes 98312 | tf_op jit(solution)/shard_map/ppermute | solution.py:19
  10.5 1.0 copy-start.2
  10.5 2.4 copy-start
  13.9 9.6 %collective-permute-start.2 = (f32[16,1,2048]{2,0,1:T(8,128)S(1)}, f32[16,1,2048]{2,0,1:T(8,128)S(1)}, u32[]{:S(2)}, u32[]{:S(2)}) collective-permute-start(f32[16,1,2048]{2,0,1:T(8,128)S(1)} %get-tuple-element.41), channel_id=1, source_target_pairs={{0,4},{4,8},{8,12},{12,16},{16,20},{20,24},{24,28},{28,32},{32,36}... | collective-permute-start | bytes 393224 | tf_op jit(solution)/shard_map/ppermute | solution.py:18
  15.8 9.5 %collective-permute-start.3 = (f32[16,1,2048]{2,0,1:T(8,128)S(1)}, f32[16,1,2048]{2,0,1:T(8,128)S(1)}, u32[]{:S(2)}, u32[]{:S(2)}) collective-permute-start(f32[16,1,2048]{2,0,1:T(8,128)S(1)} %get-tuple-element.42), channel_id=1, source_target_pairs={{4,0},{8,4},{12,8},{16,12},{20,16},{24,20},{28,24},{32,28},{36,32}... | collective-permute-start | bytes 393224 | tf_op jit(solution)/shard_map/ppermute | solution.py:19
  27.3 9.7 %collective-permute-start.4 = (f32[16,1,2048]{2,0,1:T(8,128)S(1)}, f32[16,1,2048]{2,0,1:T(8,128)S(1)}, u32[]{:S(2)}, u32[]{:S(2)}) collective-permute-start(f32[16,1,2048]{2,0,1:T(8,128)S(1)} %get-tuple-element.35), channel_id=1, source_target_pairs={{0,4},{4,8},{8,12},{12,16},{16,20},{20,24},{24,28},{28,32},{32,36}... | collective-permute-start | bytes 393224 | tf_op jit(solution)/shard_map/ppermute | solution.py:18
  29.2 9.6 %collective-permute-start.5 = (f32[16,1,2048]{2,0,1:T(8,128)S(1)}, f32[16,1,2048]{2,0,1:T(8,128)S(1)}, u32[]{:S(2)}, u32[]{:S(2)}) collective-permute-start(f32[16,1,2048]{2,0,1:T(8,128)S(1)} %get-tuple-element.36), channel_id=1, source_target_pairs={{4,0},{8,4},{12,8},{16,12},{20,16},{24,20},{28,24},{32,28},{36,32}... | collective-permute-start | bytes 393224 | tf_op jit(solution)/shard_map/ppermute | solution.py:19
  40.8 9.7 %collective-permute-start.6 = (f32[16,1,2048]{2,0,1:T(8,128)S(1)}, f32[16,1,2048]{2,0,1:T(8,128)S(1)}, u32[]{:S(2)}, u32[]{:S(2)}) collective-permute-start(f32[16,1,2048]{2,0,1:T(8,128)S(1)} %get-tuple-element.29), channel_id=1, source_target_pairs={{0,4},{4,8},{8,12},{12,16},{16,20},{20,24},{24,28},{28,32},{32,36}... | collective-permute-start | bytes 393224 | tf_op jit(solution)/shard_map/ppermute | solution.py:18
  42.8 9.6 %collective-permute-start.7 = (f32[16,1,2048]{2,0,1:T(8,128)S(1)}, f32[16,1,2048]{2,0,1:T(8,128)S(1)}, u32[]{:S(2)}, u32[]{:S(2)}) collective-permute-start(f32[16,1,2048]{2,0,1:T(8,128)S(1)} %get-tuple-element.30), channel_id=1, source_target_pairs={{4,0},{8,4},{12,8},{16,12},{20,16},{24,20},{28,24},{32,28},{36,32}... | collective-permute-start | bytes 393224 | tf_op jit(solution)/shard_map/ppermute | solution.py:19
  54.4 9.7 %collective-permute-start.8 = (f32[16,1,2048]{2,0,1:T(8,128)S(1)}, f32[16,1,2048]{2,0,1:T(8,128)S(1)}, u32[]{:S(2)}, u32[]{:S(2)}) collective-permute-start(f32[16,1,2048]{2,0,1:T(8,128)S(1)} %get-tuple-element.23), channel_id=1, source_target_pairs={{0,4},{4,8},{8,12},{12,16},{16,20},{20,24},{24,28},{28,32},{32,36}... | collective-permute-start | bytes 393224 | tf_op jit(solution)/shard_map/ppermute | solution.py:18
  56.3 9.6 %collective-permute-start.9 = (f32[16,1,2048]{2,0,1:T(8,128)S(1)}, f32[16,1,2048]{2,0,1:T(8,128)S(1)}, u32[]{:S(2)}, u32[]{:S(2)}) collective-permute-start(f32[16,1,2048]{2,0,1:T(8,128)S(1)} %get-tuple-element.24), channel_id=1, source_target_pairs={{4,0},{8,4},{12,8},{16,12},{20,16},{24,20},{28,24},{32,28},{36,32}... | collective-permute-start | bytes 393224 | tf_op jit(solution)/shard_map/ppermute | solution.py:19
  67.6 11.1 %collective-permute-start.10 = (f32[16,4,2048]{2,0,1:T(8,128)S(1)}, f32[16,4,2048]{2,0,1:T(8,128)S(1)}, u32[]{:S(2)}, u32[]{:S(2)}) collective-permute-start(f32[16,4,2048]{2,0,1:T(8,128)S(1)} %get-tuple-element.18), channel_id=1, source_target_pairs={{0,1},{1,0},{2,3},{3,2},{4,5},{5,4},{6,7},{7,6},{8,9},{9,8},{10,11... | collective-permute-start | bytes 1572872 | tf_op jit(solution)/shard_map/ppermute | solution.py:25
  576.0 5.6 collective-permute-start.11
  589.6 11.1 %collective-permute-start.12 = (f32[16,4,2048]{2,0,1:T(8,128)S(1)}, f32[16,4,2048]{2,0,1:T(8,128)S(1)}, u32[]{:S(2)}, u32[]{:S(2)}) collective-permute-start(f32[16,4,2048]{2,0,1:T(8,128)S(1)} %get-tuple-element.16), channel_id=1, source_target_pairs={{0,1},{1,0},{2,3},{3,2},{4,5},{5,4},{6,7},{7,6},{8,9},{9,8},{10,11... | collective-permute-start | bytes 1572872 | tf_op jit(solution)/shard_map/ppermute | solution.py:25
where the time goes:
time: 603 us; the launch traced here: 602 us
  blocking collectives  496 us (82%)
  starting transfers between devices  53.2 us (9%)
  waiting for transfers between devices  27.7 us (5%)
  other arithmetic  16.6 us (3%)
    psum x1, blocking collectives, per_device(): tile_sum = lax.psum(partial_value, 'tile')  496 us
    ppermute x5, starting transfers between devices, padded(): after = lax.ppermute(initial, axis, down)  35.2 us
    ppermute x3, waiting for transfers between devices, swapped(): lax.ppermute(value, axis, [(i, i ^ 1 << apart) for i in range(lax.axis_si...  19.2 us
  transfers between devices with their start and end apart: 13, of which 11 were waited for; matrix products, arithmetic and copies ran while one was open for 0% of the time, Pallas kernels for 0%

commit v1 on v0

--- a/solution.py
+++ b/solution.py
@@ -110,7 +110,8 @@
     )
     matrix = merged.reshape(column_count, -1)
     partial_value = gram_of(matrix)
-    tile_sum = lax.psum(partial_value, "tile")
+    parts = lax.all_gather(partial_value, "tile")
+    tile_sum = jnp.sum(parts, axis=0)
     total = tile_sum + swapped(tile_sum, "fac", 0)
     lower_factor = jnp.linalg.cholesky(total / ncells)
     ortho = lax.linalg.triangular_solve(lower_factor, matrix, left_side=True, lower=True).reshape(

time: 603 us -> 220 us (0.36)
  the two profiles are of different devices: /device:TPU:262 before, /device:TPU:2 now
where the time goes in v1:
time: 220 us; the launch traced here: 219 us
  blocking collectives  124 us (56%)
  starting transfers between devices  37.4 us (17%)
  waiting for transfers between devices  31.2 us (14%)
  other arithmetic  17.7 us (8%)
  local copies, waits for them, and re-layouts  6.37 us (3%)
    all_gather x1, blocking collectives, per_device(): parts = lax.all_gather(partial_value, 'tile')  124 us
    ppermute x3, waiting for transfers between devices, swapped(): lax.ppermute(value, axis, [(i, i ^ 1 << apart) for i in range(lax.axis_si...  23.8 us
    ppermute x5, starting transfers between devices, padded(): before = lax.ppermute(last, axis, up)  22.6 us
    ppermute x3, starting transfers between devices, swapped(): lax.ppermute(value, axis, [(i, i ^ 1 << apart) for i in range(lax.axis_si...  8.34 us
    ppermute x5, waiting for transfers between devices, padded(): after = lax.ppermute(initial, axis, down)  7.38 us
    add x4, other arithmetic, relax(): return (1.0 - OMEGA) * center + OMEGA * (source + beside) * inverse  6.47 us
    ppermute x5, starting transfers between devices, padded(): after = lax.ppermute(initial, axis, down)  6.46 us
  transfers between devices with their start and end apart: 13, of which 8 were waited for; matrix products, arithmetic and copies ran while one was open for 1% of the time, Pallas kernels for 0%

profile of v1, /device:TPU:2, one launch (start us, length us, event | category | flops | bytes accessed | tf_op | source)
XLA Modules:
  0.0 219.3 jit_solution(12313142447515671510)
XLA Ops:
  2.6 1.7 collective-permute-start
  6.6 1.3 fusion.69
  10.7 4.5 %collective-permute-start.2 = (f32[16,1,2048]{2,0,1:T(8,128)S(1)}, f32[16,1,2048]{2,0,1:T(8,128)S(1)}, u32[]{:S(2)}, u32[]{:S(2)}) collective-permute-start(f32[16,1,2048]{2,0,1:T(8,128)S(1)} %get-tuple-element.41), channel_id=1, source_target_pairs={{0,4},{4,8},{8,12},{12,16},{16,20},{20,24},{24,28},{28,32},{32,36}... | collective-permute-start | bytes 393224 | tf_op jit(solution)/shard_map/ppermute | solution.py:18
  17.0 1.8 collective-permute-done.3
  18.7 1.6 fusion.41
  20.7 5.5 %collective-permute-start.4 = (f32[16,1,2048]{2,0,1:T(8,128)S(1)}, f32[16,1,2048]{2,0,1:T(8,128)S(1)}, u32[]{:S(2)}, u32[]{:S(2)}) collective-permute-start(f32[16,1,2048]{2,0,1:T(8,128)S(1)} %get-tuple-element.35), channel_id=1, source_target_pairs={{0,4},{4,8},{8,12},{12,16},{16,20},{20,24},{24,28},{28,32},{32,36}... | collective-permute-start | bytes 393224 | tf_op jit(solution)/shard_map/ppermute | solution.py:18
  27.9 1.6 collective-permute-done.5
  29.4 1.6 fusion.31
  31.4 5.0 %collective-permute-start.6 = (f32[16,1,2048]{2,0,1:T(8,128)S(1)}, f32[16,1,2048]{2,0,1:T(8,128)S(1)}, u32[]{:S(2)}, u32[]{:S(2)}) collective-permute-start(f32[16,1,2048]{2,0,1:T(8,128)S(1)} %get-tuple-element.29), channel_id=1, source_target_pairs={{0,4},{4,8},{8,12},{12,16},{16,20},{20,24},{24,28},{28,32},{32,36}... | collective-permute-start | bytes 393224 | tf_op jit(solution)/shard_map/ppermute | solution.py:18
  38.1 1.6 collective-permute-done.7
  39.7 1.6 fusion.21
  41.7 5.9 %collective-permute-start.8 = (f32[16,1,2048]{2,0,1:T(8,128)S(1)}, f32[16,1,2048]{2,0,1:T(8,128)S(1)}, u32[]{:S(2)}, u32[]{:S(2)}) collective-permute-start(f32[16,1,2048]{2,0,1:T(8,128)S(1)} %get-tuple-element.23), channel_id=1, source_target_pairs={{0,4},{4,8},{8,12},{12,16},{16,20},{20,24},{24,28},{28,32},{32,36}... | collective-permute-start | bytes 393224 | tf_op jit(solution)/shard_map/ppermute | solution.py:18
  49.3 1.6 collective-permute-done.9
  50.9 1.6 fusion.11
  52.6 3.5 %collective-permute-start.10 = (f32[16,4,2048]{2,0,1:T(8,128)S(1)}, f32[16,4,2048]{2,0,1:T(8,128)S(1)}, u32[]{:S(2)}, u32[]{:S(2)}) collective-permute-start(f32[16,4,2048]{2,0,1:T(8,128)S(1)} %get-tuple-element.18), channel_id=1, source_target_pairs={{0,1},{1,0},{2,3},{3,2},{4,5},{5,4},{6,7},{7,6},{8,9},{9,8},{10,11... | collective-permute-start | bytes 1572872 | tf_op jit(solution)/shard_map/ppermute | solution.py:25
  56.1 8.3 %collective-permute-done.10 = f32[16,4,2048]{2,0,1:T(8,128)S(1)} collective-permute-done((f32[16,4,2048]{2,0,1:T(8,128)S(1)}, f32[16,4,2048]{2,0,1:T(8,128)S(1)}, u32[]{:S(2)}, u32[]{:S(2)}) %collective-permute-start.10) | collective-permute-done | bytes 524320 | tf_op jit(solution)/shard_map/ppermute | solution.py:25
  65.3 123.5 %all-gather = f32[4096,32]{1,0:T(8,128)S(1)} all-gather(f32[32,32]{1,0:T(8,128)S(1)} %convolution_bitcast_fusion), channel_id=2, replica_groups=mesh['tile'=128,'fac'=4] {'tile'}, dimensions={0}, use_global_device_ids=true | all-gather | bytes 528384 | tf_op jit(solution)/shard_map/all_gather | solution.py:113
  189.1 2.4 %collective-permute-start.11 = (f32[32,32]{0,1:T(8,128)S(1)}, f32[32,32]{0,1:T(8,128)S(1)}, u32[]{:S(2)}, u32[]{:S(2)}) collective-permute-start(f32[32,32]{0,1:T(8,128)S(1)} %copy.23), channel_id=1, source_target_pairs={{0,1},{1,0},{2,3},{3,2},{4,5},{5,4},{6,7},{7,6},{8,9},{9,8},{10,11... | collective-permute-start | bytes 12296 | tf_op jit(solution)/shard_map/ppermute | solution.py:25
  191.7 3.1 %collective-permute-done.11 = f32[32,32]{0,1:T(8,128)S(1)} collective-permute-done((f32[32,32]{0,1:T(8,128)S(1)}, f32[32,32]{0,1:T(8,128)S(1)}, u32[]{:S(2)}, u32[]{:S(2)}) %collective-permute-start.11) | collective-permute-done | bytes 4128 | tf_op jit(solution)/shard_map/ppermute | solution.py:25
  194.8 2.9 %cholesky.16 = f32[32,32]{1,0:T(8,128)S(1)} custom-call(f32[32,32]{1,0:T(8,128)S(1)} %fusion.64), custom_call_target="Cholesky" | custom-call | tf_op jit(solution)/shard_map/jit(cholesky)/cholesky | solution.py:116
  199.1 2.4 %custom-call.6 = f32[1,32,32]{1,2,0:T(8,128)S(1)} custom-call(f32[1,32,32]{2,1,0:T(8,128)S(1)} %fusion.62), custom_call_target="InvertDiagBlocksLowerTriangular" | custom-call | tf_op jit(solution)/shard_map/triangular_solve | solution.py:117
  202.7 2.4 %collective-permute-start.12 = (f32[16,4,2048]{2,0,1:T(8,128)S(1)}, f32[16,4,2048]{2,0,1:T(8,128)S(1)}, u32[]{:S(2)}, u32[]{:S(2)}) collective-permute-start(f32[16,4,2048]{2,0,1:T(8,128)S(1)} %get-tuple-element.16), channel_id=1, source_target_pairs={{0,1},{1,0},{2,3},{3,2},{4,5},{5,4},{6,7},{7,6},{8,9},{9,8},{10,11... | collective-permute-start | bytes 1572872 | tf_op jit(solution)/shard_map/ppermute | solution.py:25
  205.1 12.5 %collective-permute-done.12 = f32[16,4,2048]{2,0,1:T(8,128)S(1)} collective-permute-done((f32[16,4,2048]{2,0,1:T(8,128)S(1)}, f32[16,4,2048]{2,0,1:T(8,128)S(1)}, u32[]{:S(2)}, u32[]{:S(2)}) %collective-permute-start.12) | collective-permute-done | bytes 524320 | tf_op jit(solution)/shard_map/ppermute | solution.py:25
  217.7 1.6 copy.29
  (53 shorter events, 18.7 us)
Async XLA Ops:
  0.0 9.7 %copy-start = (f32[16,8,2048]{2,1,0:T(8,128)S(1)}, f32[16,8,2048]{2,1,0:T(8,128)}, u32[]{:S(2)}) copy-start(f32[16,8,2048]{2,1,0:T(8,128)} %param.5) | copy-start | bytes 3145732
  2.6 5.3 %collective-permute-start = (f32[4,1,2048]{2,1,0:T(1,128)S(1)}, f32[4,1,2048]{2,1,0:T(1,128)S(1)}, u32[]{:S(2)}, u32[]{:S(2)}) collective-permute-start(f32[4,1,2048]{2,1,0:T(1,128)S(1)} %get-tuple-element.43), channel_id=1, source_target_pairs={{0,4},{4,8},{8,12},{12,16},{16,20},{20,24},{24,28},{28,32},{32,36}... | collective-permute-start | bytes 98312 | tf_op jit(solution)/shard_map/ppermute | solution.py:18
  4.4 4.5 %collective-permute-start.1 = (f32[4,1,2048]{2,1,0:T(1,128)S(1)}, f32[4,1,2048]{2,1,0:T(1,128)S(1)}, u32[]{:S(2)}, u32[]{:S(2)}) collective-permute-start(f32[4,1,2048]{2,1,0:T(1,128)S(1)} %get-tuple-element.44), channel_id=1, source_target_pairs={{4,0},{8,4},{12,8},{16,12},{20,16},{24,20},{28,24},{32,28},{36,32}... | collective-permute-start | bytes 98312 | tf_op jit(solution)/shard_map/ppermute | solution.py:19
  10.7 6.2 %collective-permute-start.2 = (f32[16,1,2048]{2,0,1:T(8,128)S(1)}, f32[16,1,2048]{2,0,1:T(8,128)S(1)}, u32[]{:S(2)}, u32[]{:S(2)}) collective-permute-start(f32[16,1,2048]{2,0,1:T(8,128)S(1)} %get-tuple-element.41), channel_id=1, source_target_pairs={{0,4},{4,8},{8,12},{12,16},{16,20},{20,24},{24,28},{28,32},{32,36}... | collective-permute-start | bytes 393224 | tf_op jit(solution)/shard_map/ppermute | solution.py:18
  15.3 3.4 %collective-permute-start.3 = (f32[16,1,2048]{2,0,1:T(8,128)S(1)}, f32[16,1,2048]{2,0,1:T(8,128)S(1)}, u32[]{:S(2)}, u32[]{:S(2)}) collective-permute-start(f32[16,1,2048]{2,0,1:T(8,128)S(1)} %get-tuple-element.42), channel_id=1, source_target_pairs={{4,0},{8,4},{12,8},{16,12},{20,16},{24,20},{28,24},{32,28},{36,32}... | collective-permute-start | bytes 393224 | tf_op jit(solution)/shard_map/ppermute | solution.py:19
  20.7 7.1 %collective-permute-start.4 = (f32[16,1,2048]{2,0,1:T(8,128)S(1)}, f32[16,1,2048]{2,0,1:T(8,128)S(1)}, u32[]{:S(2)}, u32[]{:S(2)}) collective-permute-start(f32[16,1,2048]{2,0,1:T(8,128)S(1)} %get-tuple-element.35), channel_id=1, source_target_pairs={{0,4},{4,8},{8,12},{12,16},{16,20},{20,24},{24,28},{28,32},{32,36}... | collective-permute-start | bytes 393224 | tf_op jit(solution)/shard_map/ppermute | solution.py:18
  26.2 3.2 %collective-permute-start.5 = (f32[16,1,2048]{2,0,1:T(8,128)S(1)}, f32[16,1,2048]{2,0,1:T(8,128)S(1)}, u32[]{:S(2)}, u32[]{:S(2)}) collective-permute-start(f32[16,1,2048]{2,0,1:T(8,128)S(1)} %get-tuple-element.36), channel_id=1, source_target_pairs={{4,0},{8,4},{12,8},{16,12},{20,16},{24,20},{28,24},{32,28},{36,32}... | collective-permute-start | bytes 393224 | tf_op jit(solution)/shard_map/ppermute | solution.py:19
  31.4 6.6 %collective-permute-start.6 = (f32[16,1,2048]{2,0,1:T(8,128)S(1)}, f32[16,1,2048]{2,0,1:T(8,128)S(1)}, u32[]{:S(2)}, u32[]{:S(2)}) collective-permute-start(f32[16,1,2048]{2,0,1:T(8,128)S(1)} %get-tuple-element.29), channel_id=1, source_target_pairs={{0,4},{4,8},{8,12},{12,16},{16,20},{20,24},{24,28},{28,32},{32,36}... | collective-permute-start | bytes 393224 | tf_op jit(solution)/shard_map/ppermute | solution.py:18
  36.4 3.2 %collective-permute-start.7 = (f32[16,1,2048]{2,0,1:T(8,128)S(1)}, f32[16,1,2048]{2,0,1:T(8,128)S(1)}, u32[]{:S(2)}, u32[]{:S(2)}) collective-permute-start(f32[16,1,2048]{2,0,1:T(8,128)S(1)} %get-tuple-element.30), channel_id=1, source_target_pairs={{4,0},{8,4},{12,8},{16,12},{20,16},{24,20},{28,24},{32,28},{36,32}... | collective-permute-start | bytes 393224 | tf_op jit(solution)/shard_map/ppermute | solution.py:19
  41.7 7.6 %collective-permute-start.8 = (f32[16,1,2048]{2,0,1:T(8,128)S(1)}, f32[16,1,2048]{2,0,1:T(8,128)S(1)}, u32[]{:S(2)}, u32[]{:S(2)}) collective-permute-start(f32[16,1,2048]{2,0,1:T(8,128)S(1)} %get-tuple-element.23), channel_id=1, source_target_pairs={{0,4},{4,8},{8,12},{12,16},{16,20},{20,24},{24,28},{28,32},{32,36}... | collective-permute-start | bytes 393224 | tf_op jit(solution)/shard_map/ppermute | solution.py:18
  47.6 3.2 %collective-permute-start.9 = (f32[16,1,2048]{2,0,1:T(8,128)S(1)}, f32[16,1,2048]{2,0,1:T(8,128)S(1)}, u32[]{:S(2)}, u32[]{:S(2)}) collective-permute-start(f32[16,1,2048]{2,0,1:T(8,128)S(1)} %get-tuple-element.24), channel_id=1, source_target_pairs={{4,0},{8,4},{12,8},{16,12},{20,16},{24,20},{28,24},{32,28},{36,32}... | collective-permute-start | bytes 393224 | tf_op jit(solution)/shard_map/ppermute | solution.py:19
  52.6 11.8 %collective-permute-start.10 = (f32[16,4,2048]{2,0,1:T(8,128)S(1)}, f32[16,4,2048]{2,0,1:T(8,128)S(1)}, u32[]{:S(2)}, u32[]{:S(2)}) collective-permute-start(f32[16,4,2048]{2,0,1:T(8,128)S(1)} %get-tuple-element.18), channel_id=1, source_target_pairs={{0,1},{1,0},{2,3},{3,2},{4,5},{5,4},{6,7},{7,6},{8,9},{9,8},{10,11... | collective-permute-start | bytes 1572872 | tf_op jit(solution)/shard_map/ppermute | solution.py:25
  189.1 5.6 %collective-permute-start.11 = (f32[32,32]{0,1:T(8,128)S(1)}, f32[32,32]{0,1:T(8,128)S(1)}, u32[]{:S(2)}, u32[]{:S(2)}) collective-permute-start(f32[32,32]{0,1:T(8,128)S(1)} %copy.23), channel_id=1, source_target_pairs={{0,1},{1,0},{2,3},{3,2},{4,5},{5,4},{6,7},{7,6},{8,9},{9,8},{10,11... | collective-permute-start | bytes 12296 | tf_op jit(solution)/shard_map/ppermute | solution.py:25
  202.7 14.9 %collective-permute-start.12 = (f32[16,4,2048]{2,0,1:T(8,128)S(1)}, f32[16,4,2048]{2,0,1:T(8,128)S(1)}, u32[]{:S(2)}, u32[]{:S(2)}) collective-permute-start(f32[16,4,2048]{2,0,1:T(8,128)S(1)} %get-tuple-element.16), channel_id=1, source_target_pairs={{0,1},{1,0},{2,3},{3,2},{4,5},{5,4},{6,7},{7,6},{8,9},{9,8},{10,11... | collective-permute-start | bytes 1572872 | tf_op jit(solution)/shard_map/ppermute | solution.py:25
